TPU v7x, 32 devices: a whole 2x2x4 slice. The times are simulated.
32 devices in a mesh: freq: 8 (over z, x), panel: 4 (over y, core).
Axes of the slice: x: 2, y: 2, z: 4, core: 2. Of those that a mesh axis runs over, the one named last changes fastest.
Arguments:
- wavefield: float32 [8, 2, 128, 4096], P('freq', None, None, 'panel'), may hold values from -6 to 6
- direct: float32 [8, 2, 128, 4096], P('freq', None, None, 'panel'), may hold values from -6 to 6
- left_factors: float32 [8, 4096, 6, 128], P('freq', 'panel'), may hold values from -0.375 to 0.375
- right_factors: float32 [8, 16, 6, 256, 128], P('freq', 'panel'), may hold values from -0.3125 to 0.3125
- tile_src: int32 [16, 6], P('panel'), may hold values from -1 to 7, as said below
- onset: int32 [128, 2048], P('freq'), may hold values from 128 to 895
Outputs:
- focusing: float32 [8, 2, 128, 4096], P('freq', None, None, 'panel')
Inputs may be any that keep to these rules, and one draw needn't show every extreme that they name: `tile_src`: in each receiver panel's row the first k slots name distinct source tiles, with 2 <= k <= 6, and the other slots hold -1; in every aligned block of 4 panels at least one panel fills all 6 slots.
All inputs are finite; a program needn't handle non-finite values.
Results may differ from a plain program's by a relative error of at most 0.0003.
Values sent between devices are 32-bit elements; how exact they have to be, the bound alone decides.
A program may use at most 128 MiB of HBM per device.

v0:
```python
import functools
import math

import jax
import jax.numpy as jnp
from jax import lax
from jax.experimental import pallas as pl
from jax.experimental.pallas import tpu as pltpu
from jax.sharding import PartitionSpec as P

NT = 1024
FIRST_BIN = 8
SRC_TILES = 8
LANES = 128
BF16 = jnp.bfloat16
F32 = jnp.float32
NN = (((1,), (0,)), ((), ()))
NT_DIMS = (((1,), (1,)), ((), ()))


def split(x):
    high = x.astype(BF16)
    return high, (x - high.astype(F32)).astype(BF16)


def mxu(a, b, dims):
    return lax.dot_general(a, b, dims, preferred_element_type=F32)


def lanes(*parts):
    return jnp.concatenate(parts, axis=1)


def pair_coef(products):
    rows, width = products.shape
    first, second = products[: rows // 2], products[rows // 2 :]
    lane = lax.broadcasted_iota(jnp.int32, first.shape, 1)
    sign = jnp.where(lane < width // 2, 1.0, -1.0).astype(F32)
    swap = lambda x: pltpu.roll(x, width // 2, 1)
    return jnp.concatenate([first + sign * swap(second), second - sign * swap(first)], axis=0)

def gate_tables(count):
    assert 2 * (FIRST_BIN + count - 1) < NT
    cot = lambda m: 1.0 / math.tan(math.pi * m / NT)
    minus = [[0.0 if f == g else cot(g - f) for g in range(count)] for f in range(count)]
    plus = [[cot(f + g + 2 * FIRST_BIN) for g in range(count)] for f in range(count)]
    real = [[0.5 * (minus[f][g] + plus[f][g]) for g in range(count)] for f in range(count)]
    imag = [[0.5 * (plus[f][g] - minus[f][g]) for g in range(count)] for f in range(count)]
    return real, imag


def gate_map(xr, xi, tables):
    real, imag = tables
    count = len(xr)
    total = functools.reduce(lambda a, b: a + b, xr)
    gr, gi = [], []
    for f in range(count):
        a = 0.5 * xr[f] - total
        b = 0.5 * xi[f]
        for g in range(count):
            a = a + real[f][g] * xi[g]
            b = b + imag[f][g] * xr[g]
        gr.append(a)
        gi.append(b)
    return gr, gi


def gate(xr, xi, c1, s1, mark, tables):
    count = len(xr)
    scale = 0.5 / math.sqrt(count * NT)
    ec, es = c1, s1
    power = 1
    while power * 2 <= FIRST_BIN:
        ec, es = ec * ec - es * es, 2.0 * ec * es
        power *= 2
    while power < FIRST_BIN:
        ec, es = ec * c1 - es * s1, ec * s1 + es * c1
        power += 1
    cs, sn = [], []
    for f in range(count):
        cs.append(ec)
        sn.append(es)
        ec, es = ec * c1 - es * s1, ec * s1 + es * c1
    yr = [xr[f] * cs[f] - xi[f] * sn[f] for f in range(count)]
    yi = [xr[f] * sn[f] + xi[f] * cs[f] for f in range(count)]
    hr, hi = gate_map(yr, yi, tables)
    gr, gi = gate_map(xr, xi, tables)
    br = [scale * (cs[f] * hr[f] + sn[f] * hi[f] - gr[f] + mark * xr[f]) for f in range(count)]
    bi = [scale * (cs[f] * hi[f] - sn[f] * hr[f] - gi[f] + mark * xi[f]) for f in range(count)]
    return br, bi


def unit(mark):
    quarter = NT // 4
    phase = mark & (NT - 1)
    quad = lax.shift_right_logical(phase + quarter // 2, quarter.bit_length() - 1)
    x = (2.0 * math.pi / NT) * (phase - quad * quarter).astype(F32)
    z = x * x
    c = jnp.full_like(x, 1.0 / math.factorial(10))
    s = jnp.full_like(x, 1.0 / math.factorial(11))
    for n in (8, 6, 4, 2, 0):
        c = 1.0 / math.factorial(n) - z * c
    for n in (9, 7, 5, 3, 1):
        s = 1.0 / math.factorial(n) - z * s
    s = s * x
    quad = quad & 3
    swap = (quad & 1) == 1
    cos = jnp.where(swap, s, c)
    sin = jnp.where(swap, c, s)
    cos = jnp.where((quad == 1) | (quad == 2), -cos, cos)
    sin = jnp.where(quad >= 2, -sin, sin)
    return cos, sin


def marchenko_kernel(
    nf, ny, chunks, tile_ref, onset_ref, field_hbm, direct_hbm, left_hbm, right_hbm, out_hbm,
    field, direct, left, right, coef_h, coef_l, left_h, left_l, right_h, right_l,
    part, buf1, sums, buf2, xbuf, rbuf, obuf, source, chosen_ref,
    field_sem, direct_sem, left_sem, right_sem, out_sem,
    s1s, s1r, s2s, s2r, s3s, s3r, s4s, s4r, s5s, s5r, s6s, s6r,
):
    tables = gate_tables(nf)
    panels, slots, rows, width = right.shape
    pair = part.shape[1]
    virtual = pair // 2
    vp = virtual // nf
    blocks = rows // LANES
    np_ = 2 * ny
    tiles = np_ // blocks
    me = lax.axis_index("freq")
    q = lax.axis_index("panel")
    y, c = q // 2, q % 2
    partner = {"panel": y * 2 + 1 - c}
    ypeer = [{"panel": ((y + d) % ny) * 2 + c} for d in range(ny)]
    fpeer = [{"freq": (me + d) % nf} for d in range(nf)]
    MESH = pl.DeviceIdType.MESH

    loads_a, loads_b, loads_c = [], [], []
    for p in range(panels):
        cols = pl.ds(p * rows, rows)
        loads_a.append(pltpu.make_async_copy(field_hbm.at[:, :, cols], field.at[p], field_sem.at[p]))
        loads_a.append(pltpu.make_async_copy(left_hbm.at[:, cols, :], left.at[p], left_sem.at[p]))
        loads_b.append(pltpu.make_async_copy(right_hbm.at[p], right.at[p], right_sem.at[p]))
        loads_c.append(pltpu.make_async_copy(direct_hbm.at[:, :, cols], direct.at[p], direct_sem.at[p]))
    for copy in loads_a + loads_b + loads_c:
        copy.start()

    barrier = pltpu.get_barrier_semaphore()
    for dev in [partner] + ypeer[1:] + fpeer[1:]:
        pl.semaphore_signal(barrier, inc=1, device_id=dev, device_id_type=MESH)

    def slot_of(p, j):
        slot = jnp.int32(slots)
        for s in range(slots):
            slot = jnp.where(tile_ref[p, s] == j, jnp.int32(s), slot)
        return slot

    zero = jnp.zeros((pair, width), BF16)
    for p in range(panels):
        coef_h[p, slots] = zero
        coef_l[p, slots] = zero
        left_h[p, slots] = zero[:rows]
        left_l[p, slots] = zero[:rows]

    for p in range(panels):
        loads_a[2 * p].wait()
        loads_a[2 * p + 1].wait()
        fh, fl = split(field[p].reshape(pair, rows))
        fcat = lanes(fh, fh, fl)
        for s in range(0, slots, 2):
            halves = []
            for i in range(2):
                h, l = split(left[p, s + i])
                left_h[p, s + i] = h
                left_l[p, s + i] = l
                halves.append(jnp.concatenate([h, l, h], axis=0))
            products = mxu(fcat, lanes(*halves), NN)
            for i in range(2):
                h, l = split(pair_coef(products[:, i * width : (i + 1) * width]))
                coef_h[p, s + i] = h
                coef_l[p, s + i] = l
    for p in range(panels):
        loads_b[p].wait()
        for s in range(slots):
            h, l = split(right[p, s])
            right_h[p, s] = h
            right_l[p, s] = l

    def send(src, dst, ssem, rsem, device):
        copy = pltpu.make_async_remote_copy(
            src_ref=src, dst_ref=dst, send_sem=ssem, recv_sem=rsem, device_id=device, device_id_type=MESH
        )
        copy.start()
        return copy

    def block(yy, cc, ch):
        return ch * np_ + yy * 2 + cc

    order = list(range(1, ny)) + [0]
    c1 = [[None] * ny for _ in range(chunks)]
    c2 = [[None] * ny for _ in range(chunks)]
    c3 = [[None] * nf for _ in range(chunks)]
    c4 = [[None] * nf for _ in range(chunks)]
    c5 = [[None] * ny for _ in range(chunks)]
    c6 = [[None] * ny for _ in range(chunks)]

    def stage_adjoint(ch):
        for j in range(ch * tiles, (ch + 1) * tiles):
            ins, outs = [], []
            for p in range(panels):
                slot = slot_of(p, j)
                real = jnp.minimum(slot, slots - 1)
                h, l = coef_h[p, slot], coef_l[p, slot]
                rh, rl = right_h[p, real], right_l[p, real]
                ins += [h, l, h]
                outs += [rh, rh, rl]
            tile = mxu(lanes(*ins), lanes(*outs), NT_DIMS)
            for b in range(blocks):
                part[j * blocks + b] = tile[:, b * LANES : (b + 1) * LANES]
        if ch == 0:
            pl.semaphore_wait(barrier, 1 + (ny - 1) + (nf - 1))
        for d in order:
            c1[ch][d] = send(
                part.at[block((y + d) % ny, 1 - c, ch)], buf1.at[ch, d], s1s.at[ch, d], s1r.at[ch, d], partner
            )

    def stage_sum(ch):
        for d in order:
            c1[ch][d].wait_recv()
            sums[ch, d] = part[block((y + d) % ny, c, ch)] + buf1[ch, d]
            if d:
                c2[ch][d] = send(sums.at[ch, d], buf2.at[ch, d - 1], s2s.at[ch, d], s2r.at[ch, d], ypeer[d])

    def stage_out(ch):
        total = sums[ch, 0]
        for d in range(1, ny):
            c2[ch][d].wait_recv()
            total = total + buf2[ch, d - 1]
        if vp % 8 == 0:
            xbuf[ch] = total.reshape(2, nf, vp, LANES)
        else:
            for k in range(2 * nf):
                xbuf[ch, k // nf, k % nf] = total[k * vp : (k + 1) * vp]
        for d in range(1, nf):
            to = (me + d) % nf
            c3[ch][d] = send(xbuf.at[ch, :, to], rbuf.at[ch, me], s3s.at[ch, d], s3r.at[ch, d], fpeer[d])
        rbuf[ch, me] = xbuf[ch, :, me]

    def stage_gate(ch):
        at = block(y, c, ch)
        mark = onset_ref[:, pl.ds(pl.multiple_of(at * LANES, LANES), LANES)]
        cos, sin = unit(mark)
        for d in range(1, nf):
            c3[ch][d].wait_recv()
        xr = [rbuf[ch, f, 0] for f in range(nf)]
        xi = [rbuf[ch, f, 1] for f in range(nf)]
        br, bi = gate(xr, xi, cos, sin, mark.astype(F32), tables)
        for f in range(nf):
            obuf[ch, f, 0] = br[f]
            obuf[ch, f, 1] = bi[f]
        for d in range(1, nf):
            to = (me + d) % nf
            c4[ch][d] = send(obuf.at[ch, to], source.at[at, :, me], s4s.at[ch, d], s4r.at[ch, d], fpeer[d])
        source[at, :, me] = obuf[ch, me]

    def stage_back(ch):
        for d in range(1, nf):
            c4[ch][d].wait_recv()
        at = source.at[block(y, c, ch)]
        for d in range(1, ny):
            c5[ch][d] = send(at, at, s5s.at[ch, d], s5r.at[ch, d], ypeer[d])
        c6[ch][0] = send(at, at, s6s.at[ch, 0], s6r.at[ch, 0], partner)

    def stage_pass(ch):
        for d in range(1, ny):
            c5[ch][d].wait_recv()
            at = source.at[block((y + ny - d) % ny, c, ch)]
            c6[ch][d] = send(at, at, s6s.at[ch, d], s6r.at[ch, d], partner)

    def load_block(b):
        if vp % 8 == 0:
            return source[b].reshape(pair, LANES)
        for k in range(2 * nf):
            chosen_ref[k * vp : (k + 1) * vp, :] = source[b, k // nf, k % nf]
        return chosen_ref[...]

    stores = []

    def stage_forward(ch):
        for d in range(ny):
            c6[ch][d].wait_recv()
        left_in = [[] for _ in range(panels)]
        left_w = [[] for _ in range(panels)]
        for j in range(ch * tiles, (ch + 1) * tiles):
            h, l = split(lanes(*[load_block(j * blocks + b) for b in range(blocks)]))
            at = [slot_of(p, j) for p in range(panels)]
            real = [jnp.minimum(a, slots - 1) for a in at]
            rh = lanes(*[right_h[p, real[p]] for p in range(panels)])
            rl = lanes(*[right_l[p, real[p]] for p in range(panels)])
            products = mxu(lanes(h, h, l), jnp.concatenate([rh, rl, rh], axis=0), NN)
            for p in range(panels):
                ph, plow = split(pair_coef(products[:, p * width : (p + 1) * width]))
                lh, ll = left_h[p, at[p]], left_l[p, at[p]]
                left_in[p] += [ph, ph, plow]
                left_w[p] += [lh, ll, lh]
        for p in range(panels):
            if ch == 0:
                loads_c[p].wait()
            total = mxu(lanes(*left_in[p]), lanes(*left_w[p]), NT_DIMS)
            direct[p] -= total.reshape(2, virtual, rows)
            if ch == chunks - 1:
                store = pltpu.make_async_copy(
                    direct.at[p], out_hbm.at[:, :, pl.ds(p * rows, rows)], out_sem.at[p]
                )
                store.start()
                stores.append(store)

    for ch in range(chunks):
        stage_adjoint(ch)
        if ch:
            stage_sum(ch - 1)
    stage_sum(chunks - 1)
    stages = [(stage_gate, 2), (stage_out, 0), (stage_back, 3), (stage_pass, 5), (stage_forward, 6)]
    for step in range(chunks + 6):
        for stage, lag in stages:
            if 0 <= step - lag < chunks:
                stage(step - lag)
    for group in (c1, c2, c3, c4, c5, c6):
        for ch in range(chunks):
            for copy in group[ch]:
                if copy is not None:
                    copy.wait_send()
    for store in stores:
        store.wait()


def shards(nf, npanel, wavefield, direct, left_factors, right_factors, tile_src, onset):
    panels, slots = tile_src.shape
    rows, width = right_factors.shape[3:]
    virtual = wavefield.shape[2]
    blocks = SRC_TILES * rows // LANES
    chunks = blocks // npanel
    ny = npanel // 2
    vp = virtual // nf
    pair = 2 * virtual
    left = jnp.transpose(left_factors[0], (1, 0, 2))
    hbm = pl.BlockSpec(memory_space=pl.ANY)
    dma = lambda n: [pltpu.SemaphoreType.DMA((chunks, n))] * 2
    split_buf = lambda n, r: [pltpu.VMEM((panels, n, r, width), BF16)] * 2
    out = pl.pallas_call(
        functools.partial(marchenko_kernel, nf, ny, chunks),
        in_specs=[
            pl.BlockSpec(memory_space=pltpu.SMEM), pl.BlockSpec(memory_space=pltpu.VMEM), hbm, hbm, hbm, hbm,
        ],
        out_specs=hbm,
        out_shape=jax.ShapeDtypeStruct(direct.shape[1:], F32),
        scratch_shapes=[
            pltpu.VMEM((panels, 2, virtual, rows), F32),
            pltpu.VMEM((panels, 2, virtual, rows), F32),
            pltpu.VMEM((panels, slots, rows, width), F32),
            pltpu.VMEM((panels, slots, rows, width), F32),
            *split_buf(slots + 1, pair),
            *split_buf(slots + 1, rows),
            *split_buf(slots, rows),
            pltpu.VMEM((blocks, pair, LANES), F32),
            pltpu.VMEM((chunks, ny, pair, LANES), F32),
            pltpu.VMEM((chunks, ny, pair, LANES), F32),
            pltpu.VMEM((chunks, ny - 1, pair, LANES), F32),
            pltpu.VMEM((chunks, 2, nf, vp, LANES), F32),
            pltpu.VMEM((chunks, nf, 2, vp, LANES), F32),
            pltpu.VMEM((chunks, nf, 2, vp, LANES), F32),
            pltpu.VMEM((blocks, 2, nf, vp, LANES), F32),
            pltpu.VMEM((pair, LANES), F32),
            *[pltpu.SemaphoreType.DMA((panels,))] * 5,
            *dma(ny), *dma(ny), *dma(nf), *dma(nf), *dma(ny), *dma(ny),
        ],
        compiler_params=pltpu.CompilerParams(collective_id=0, has_side_effects=True),
        name="marchenko",
    )(tile_src, onset, wavefield[0], direct[0], left, right_factors[0])
    return out[None]


def solution(mesh):
    in_specs = (
        P("freq", None, None, "panel"),
        P("freq", None, None, "panel"),
        P("freq", "panel", None, None),
        P("freq", "panel", None, None, None),
        P("panel", None),
        P("freq", None),
    )
    out_specs = P("freq", None, None, "panel")
    body = functools.partial(shards, mesh.shape["freq"], mesh.shape["panel"])
    return jax.shard_map(body, mesh=mesh, in_specs=in_specs, out_specs=out_specs, check_vma=False)
```

profile of v0, /device:TPU:1, one launch (start us, length us, event | category | flops | bytes accessed | tf_op | source)
XLA Modules:
  0.0 50.9 jit_solution(7259954394033009636)
XLA Ops:
  0.0 48.6 %marchenko.1 = f32[2,128,1024]{2,1,0:T(8,128)} custom-call(s32[4,6]{1,0:T(4,128)} %tile_ref.1, s32[16,2048]{1,0:T(8,128)} %onset_ref.1, f32[2,128,1024]{2,1,0:T(8,128)} %bitcast.10, f32[2,128,1024]{2,1,0:T(8,128)} %bitcast.11, f32[6,1024,128]{2,1,0:T(8,128)} %bitcast.8, f32[4,6,256,128]{3,2,1,0:T(8,128)} %bitcast.9), custom_call_target="tpu_custom_call" | custom-call | tf_op jit(solution)/shard_map/marchenko/pallas_call | solution.py:350
  48.6 2.3 %copy.8 = f32[1,2,128,1024]{3,2,1,0:T(8,128)} copy(f32[1,2,128,1024]{3,2,1,0:T(8,128)} %bitcast.7) | data formatting | bytes 2097152
where the time goes:
time: 51.4 us; the launch traced here: 50.9 us
  Pallas kernels  48.6 us (95%)
  local copies, waits for them, and re-layouts  2.31 us (4%)
    pallas_call x1, Pallas kernels, shards(): pl.pallas_call(functools.partial(marchenko_kernel, nf, ny, chunks), in_sp...  48.6 us
    unnamed x1, local copies, waits for them, and re-layouts  2.31 us

commit v1 on v0

--- a/solution.py
+++ b/solution.py
@@ -113,10 +113,10 @@
 
 
 def marchenko_kernel(
-    nf, ny, chunks, tile_ref, onset_ref, field_hbm, direct_hbm, left_hbm, right_hbm, out_hbm,
+    nf, ny, chunks, tile_ref, onset_ref, field_hbm, direct_hbm, left_hbm, right_hbm, out_ref,
     field, direct, left, right, coef_h, coef_l, left_h, left_l, right_h, right_l,
     part, buf1, sums, buf2, xbuf, rbuf, obuf, source, chosen_ref,
-    field_sem, direct_sem, left_sem, right_sem, out_sem,
+    field_sem, direct_sem, left_sem, right_sem,
     s1s, s1r, s2s, s2r, s3s, s3r, s4s, s4r, s5s, s5r, s6s, s6r,
 ):
     tables = gate_tables(nf)
@@ -284,8 +284,6 @@
             chosen_ref[k * vp : (k + 1) * vp, :] = source[b, k // nf, k % nf]
         return chosen_ref[...]
 
-    stores = []
-
     def stage_forward(ch):
         for d in range(ny):
             c6[ch][d].wait_recv()
@@ -307,13 +305,11 @@
             if ch == 0:
                 loads_c[p].wait()
             total = mxu(lanes(*left_in[p]), lanes(*left_w[p]), NT_DIMS)
-            direct[p] -= total.reshape(2, virtual, rows)
+            done = direct[p] - total.reshape(2, virtual, rows)
             if ch == chunks - 1:
-                store = pltpu.make_async_copy(
-                    direct.at[p], out_hbm.at[:, :, pl.ds(p * rows, rows)], out_sem.at[p]
-                )
-                store.start()
-                stores.append(store)
+                out_ref[:, :, p * rows : (p + 1) * rows] = done
+            else:
+                direct[p] = done
 
     for ch in range(chunks):
         stage_adjoint(ch)
@@ -330,8 +326,6 @@
             for copy in group[ch]:
                 if copy is not None:
                     copy.wait_send()
-    for store in stores:
-        store.wait()
 
 
 def shards(nf, npanel, wavefield, direct, left_factors, right_factors, tile_src, onset):
@@ -352,8 +346,8 @@
         in_specs=[
             pl.BlockSpec(memory_space=pltpu.SMEM), pl.BlockSpec(memory_space=pltpu.VMEM), hbm, hbm, hbm, hbm,
         ],
-        out_specs=hbm,
-        out_shape=jax.ShapeDtypeStruct(direct.shape[1:], F32),
+        out_specs=pl.BlockSpec(memory_space=pltpu.VMEM),
+        out_shape=pltpu.VMEM(direct.shape[1:], F32),
         scratch_shapes=[
             pltpu.VMEM((panels, 2, virtual, rows), F32),
             pltpu.VMEM((panels, 2, virtual, rows), F32),
@@ -371,7 +365,7 @@
             pltpu.VMEM((chunks, nf, 2, vp, LANES), F32),
             pltpu.VMEM((blocks, 2, nf, vp, LANES), F32),
             pltpu.VMEM((pair, LANES), F32),
-            *[pltpu.SemaphoreType.DMA((panels,))] * 5,
+            *[pltpu.SemaphoreType.DMA((panels,))] * 4,
             *dma(ny), *dma(ny), *dma(nf), *dma(nf), *dma(ny), *dma(ny),
         ],
         compiler_params=pltpu.CompilerParams(collective_id=0, has_side_effects=True),

time: 51.4 us -> 49.2 us (0.957)
  local copies, waits for them, and re-layouts: 2.31 us -> 0.97 us
  Pallas kernels: 48.6 us -> 47.8 us
    unnamed x1, local copies, waits for them, and re-layouts: 2.31 us -> 0.97 us
    pallas_call x1, Pallas kernels: 48.6 us -> 47.8 us  [shards(): pl.pallas_call(functools.partial(marchenko_kernel, nf, ny, chunks), in_sp...]
where the time goes in v1:
time: 49.2 us; the launch traced here: 48.8 us
  Pallas kernels  47.8 us (97%)
  local copies, waits for them, and re-layouts  0.97 us (2%)
    pallas_call x1, Pallas kernels, shards(): pl.pallas_call(functools.partial(marchenko_kernel, nf, ny, chunks), in_sp...  47.8 us

profile of v1, /device:TPU:1, one launch (start us, length us, event | category | flops | bytes accessed | tf_op | source)
XLA Modules:
  0.0 48.8 jit_solution(2228792252888920221)
XLA Ops:
  0.0 47.8 %marchenko.1 = f32[2,128,1024]{2,1,0:T(8,128)S(1)} custom-call(s32[4,6]{1,0:T(4,128)} %tile_ref.1, s32[16,2048]{1,0:T(8,128)} %onset_ref.1, f32[2,128,1024]{2,1,0:T(8,128)} %bitcast.10, f32[2,128,1024]{2,1,0:T(8,128)} %bitcast.11, f32[6,1024,128]{2,1,0:T(8,128)} %bitcast.8, f32[4,6,256,128]{3,2,1,0:T(8,128)} %bitcast.9), custom_call_target="tpu_custom_call" | custom-call | tf_op jit(solution)/shard_map/marchenko/pallas_call | solution.py:344
  47.8 1.0 %copy.8 = f32[1,2,128,1024]{3,2,1,0:T(8,128)} copy(f32[1,2,128,1024]{3,2,1,0:T(8,128)S(1)} %bitcast.7) | data formatting | bytes 2097152

commit v2 on v1

--- a/solution.py
+++ b/solution.py
@@ -284,39 +284,41 @@
             chosen_ref[k * vp : (k + 1) * vp, :] = source[b, k // nf, k % nf]
         return chosen_ref[...]
 
-    def stage_forward(ch):
-        for d in range(ny):
-            c6[ch][d].wait_recv()
-        left_in = [[] for _ in range(panels)]
-        left_w = [[] for _ in range(panels)]
-        for j in range(ch * tiles, (ch + 1) * tiles):
-            h, l = split(lanes(*[load_block(j * blocks + b) for b in range(blocks)]))
-            at = [slot_of(p, j) for p in range(panels)]
-            real = [jnp.minimum(a, slots - 1) for a in at]
-            rh = lanes(*[right_h[p, real[p]] for p in range(panels)])
-            rl = lanes(*[right_l[p, real[p]] for p in range(panels)])
-            products = mxu(lanes(h, h, l), jnp.concatenate([rh, rl, rh], axis=0), NN)
-            for p in range(panels):
-                ph, plow = split(pair_coef(products[:, p * width : (p + 1) * width]))
-                lh, ll = left_h[p, at[p]], left_l[p, at[p]]
-                left_in[p] += [ph, ph, plow]
-                left_w[p] += [lh, ll, lh]
+    def forward(ch, d):
+        c6[ch][d].wait_recv()
+        j = ch * tiles + (y + ny - d) % ny
+        h, l = split(lanes(*[load_block(j * blocks + b) for b in range(blocks)]))
+        at = [slot_of(p, j) for p in range(panels)]
+        real = [jnp.minimum(a, slots - 1) for a in at]
+        rh = lanes(*[right_h[p, real[p]] for p in range(panels)])
+        rl = lanes(*[right_l[p, real[p]] for p in range(panels)])
+        products = mxu(lanes(h, h, l), jnp.concatenate([rh, rl, rh], axis=0), NN)
         for p in range(panels):
-            if ch == 0:
+            if ch == 0 and d == 0:
                 loads_c[p].wait()
-            total = mxu(lanes(*left_in[p]), lanes(*left_w[p]), NT_DIMS)
+            ph, plow = split(pair_coef(products[:, p * width : (p + 1) * width]))
+            lh, ll = left_h[p, at[p]], left_l[p, at[p]]
+            total = mxu(lanes(ph, ph, plow), lanes(lh, ll, lh), NT_DIMS)
             done = direct[p] - total.reshape(2, virtual, rows)
-            if ch == chunks - 1:
+            if ch == chunks - 1 and d == ny - 1:
                 out_ref[:, :, p * rows : (p + 1) * rows] = done
             else:
                 direct[p] = done
 
+    def stage_own(ch):
+        forward(ch, 0)
+
+    def stage_forward(ch):
+        for d in range(1, ny):
+            forward(ch, d)
+
+    assert blocks == 2
     for ch in range(chunks):
         stage_adjoint(ch)
         if ch:
             stage_sum(ch - 1)
     stage_sum(chunks - 1)
-    stages = [(stage_gate, 2), (stage_out, 0), (stage_back, 3), (stage_pass, 5), (stage_forward, 6)]
+    stages = [(stage_gate, 2), (stage_out, 0), (stage_back, 3), (stage_pass, 5), (stage_forward, 6), (stage_own, 4)]
     for step in range(chunks + 6):
         for stage, lag in stages:
             if 0 <= step - lag < chunks:

time: 49.2 us -> 48.6 us (0.988)
  no operation moved by 1% of the time
where the time goes in v2:
time: 48.6 us; the launch traced here: 48.5 us
  Pallas kernels  47.5 us (98%)
  local copies, waits for them, and re-layouts  0.97 us (2%)
    pallas_call x1, Pallas kernels, shards(): pl.pallas_call(functools.partial(marchenko_kernel, nf, ny, chunks), in_sp...  47.5 us
    unnamed x1, local copies, waits for them, and re-layouts  0.97 us

profile of v2, /device:TPU:1, one launch (start us, length us, event | category | flops | bytes accessed | tf_op | source)
XLA Modules:
  0.0 48.5 jit_solution(7497728980926485282)
XLA Ops:
  0.0 47.5 %marchenko.1 = f32[2,128,1024]{2,1,0:T(8,128)S(1)} custom-call(s32[4,6]{1,0:T(4,128)} %tile_ref.1, s32[16,2048]{1,0:T(8,128)} %onset_ref.1, f32[2,128,1024]{2,1,0:T(8,128)} %bitcast.10, f32[2,128,1024]{2,1,0:T(8,128)} %bitcast.11, f32[6,1024,128]{2,1,0:T(8,128)} %bitcast.8, f32[4,6,256,128]{3,2,1,0:T(8,128)} %bitcast.9), custom_call_target="tpu_custom_call" | custom-call | tf_op jit(solution)/shard_map/marchenko/pallas_call | solution.py:346
  47.5 1.0 %copy.8 = f32[1,2,128,1024]{3,2,1,0:T(8,128)} copy(f32[1,2,128,1024]{3,2,1,0:T(8,128)S(1)} %bitcast.7) | data formatting | bytes 2097152
